TPU v7x, 256 devices: a whole 4x4x8 slice. The times are simulated.
256 devices in a mesh: cuts: 64 (over x, y, z_lo), frame: 4 (over z_hi, core).
Axes of the slice: x: 4, y: 4, z: 8 (z_hi: 2, z_lo: 4; z = z_hi * 4 + z_lo), core: 2. Of those that a mesh axis runs over, the one named last changes fastest.
Arguments:
- basis: bfloat16 [2, 32, 128, 4, 256], P(None, None, 'cuts', 'frame'), may hold values from -6 to 6
- coil_maps: bfloat16 [2, 12, 128, 4, 256], P(None, None, 'cuts', 'frame'), may hold values from -3 to 3
- factors: bfloat16 [2, 32, 64], P(None, None, 'frame'), may hold values from -0.75 to 0.75
- lines: int32 [64, 128], P(None, 'cuts'), may hold values from 0 to 511
- kdata: bfloat16 [2, 64, 128, 12, 4], P(None, None, 'cuts', None, 'frame'), may hold values from -6 to 6
Outputs:
- basis_grad: float32 [2, 32, 128, 4, 256], P(None, None, 'cuts', 'frame')
- factor_grad: float32 [2, 32, 64], P(None, None, 'frame')
Inputs may be any that keep to these rules, and one draw needn't show every extreme that they name: lines[t, j] = (ky - (j // 2) * 4) * 128 + kz for a position (ky, kz) sampled in frame t whose ky lies in the rows (j // 2) * 4 to (j // 2 + 1) * 4 - 1; positions may repeat over frames.
All inputs are finite; a program needn't handle non-finite values.
Results may differ from a plain program's by a relative error of at most 0.011.
Values may be sent and summed in bfloat16 or wider, within the bound.
A program may use at most 64 MiB of HBM per device.

v0:
```python
import math
import jax
import jax.numpy as jnp
from jax import lax
from jax.sharding import PartitionSpec as P

HIGH = lax.Precision.HIGHEST


def twiddle(product, size):
    angle = product.astype(jnp.float32) * (2.0 * math.pi / size)
    factor = 1.0 / math.sqrt(size)
    return (
        (jnp.cos(angle) * factor).astype(jnp.bfloat16),
        (jnp.sin(angle) * factor).astype(jnp.bfloat16),
    )


def dft_table(size, inverse):
    index = jnp.arange(size, dtype=jnp.int32)
    product = index[:, None] * index[None, :] % size
    cosine, sine = twiddle(product, size)
    imag = sine if inverse else -sine
    return jnp.stack([jnp.stack([cosine, imag]), jnp.stack([-imag, cosine])])


def body(basis, coil_maps, factors, lines, kdata):
    n_cuts = lax.axis_size("cuts")
    slab = basis.shape[2]
    readout = basis.shape[3]
    width = basis.shape[4]
    depth = slab * n_cuts
    ky_rows = width // n_cuts
    lines_dev = lines.shape[1]
    scale = 1.0 / math.sqrt(
        coil_maps.shape[1] * lines_dev * n_cuts * readout * lax.axis_size("frame")
    )
    fwd_y = dft_table(width, False)
    inv_y = dft_table(width, True)
    every = lax.all_gather(factors, "frame", axis=2, tiled=True)
    frames = every.shape[2]
    v_re = every[0]
    v_im = every[1]
    v_re32 = v_re.astype(jnp.float32)
    v_im32 = v_im.astype(jnp.float32)
    b_re = basis[0].astype(jnp.float32)
    b_im = basis[1].astype(jnp.float32)

    def forward_hybrid(maps):
        m_re = maps[0].astype(jnp.float32)[None]
        m_im = maps[1].astype(jnp.float32)[None]
        image = jnp.stack([m_re * b_re - m_im * b_im, m_re * b_im + m_im * b_re]).astype(
            jnp.bfloat16
        )
        return jnp.einsum(
            "plzxy,pqwy->qlzxw", image, fwd_y, preferred_element_type=jnp.float32
        ).astype(jnp.bfloat16)

    def finish(back, maps, grad_acc):
        imgrad = jnp.einsum("plzxw,pqyw->qlzxy", back, inv_y, preferred_element_type=jnp.float32)
        m_re = maps[0].astype(jnp.float32)[None]
        m_im = maps[1].astype(jnp.float32)[None]
        g_re = imgrad[0]
        g_im = imgrad[1]
        return grad_acc + jnp.stack([m_re * g_re + m_im * g_im, m_re * g_im - m_im * g_re])

    fwd_z = dft_table(depth, False)
    inv_z = dft_table(depth, True).astype(jnp.float32)
    cells = depth * ky_rows
    cell_of = lines % depth * ky_rows + lines // depth
    onehot = (cell_of[:, :, None] == jnp.arange(cells, dtype=jnp.int32)[None, None, :]).astype(
        jnp.bfloat16
    )
    onehot32 = onehot.astype(jnp.float32)

    def coil_step(carry, inputs):
        grad_acc, factor_acc = carry
        maps, data = inputs
        hybrid = forward_hybrid(maps)
        moved = lax.all_to_all(hybrid, "cuts", split_axis=4, concat_axis=2, tiled=True)
        kspace = jnp.einsum("plzxr,pqkz->qlxkr", moved, fwd_z, preferred_element_type=jnp.float32)
        kspace = kspace.reshape(2, kspace.shape[1], readout, cells)
        k_re = kspace[0]
        k_im = kspace[1]
        mixed_re = jnp.einsum("lxc,lt->xtc", k_re, v_re32, precision=HIGH) - jnp.einsum(
            "lxc,lt->xtc", k_im, v_im32, precision=HIGH
        )
        mixed_im = jnp.einsum("lxc,lt->xtc", k_re, v_im32, precision=HIGH) + jnp.einsum(
            "lxc,lt->xtc", k_im, v_re32, precision=HIGH
        )
        pred_re = jnp.einsum("tsc,xtc->tsx", onehot32, mixed_re, precision=HIGH)
        pred_im = jnp.einsum("tsc,xtc->tsx", onehot32, mixed_im, precision=HIGH)
        resid = (jnp.stack([pred_re, pred_im]) - data.astype(jnp.float32)).astype(jnp.bfloat16)
        spread = jnp.einsum("qtsx,tsc->qxtc", resid, onehot, preferred_element_type=jnp.float32)
        e_re = spread[0]
        e_im = spread[1]
        gv_re = jnp.einsum("lxc,xtc->lt", k_re, e_re, precision=HIGH) + jnp.einsum(
            "lxc,xtc->lt", k_im, e_im, precision=HIGH
        )
        gv_im = jnp.einsum("lxc,xtc->lt", k_re, e_im, precision=HIGH) - jnp.einsum(
            "lxc,xtc->lt", k_im, e_re, precision=HIGH
        )
        kg_re = jnp.einsum("xtc,lt->lxc", e_re, v_re32, precision=HIGH) + jnp.einsum(
            "xtc,lt->lxc", e_im, v_im32, precision=HIGH
        )
        kg_im = jnp.einsum("xtc,lt->lxc", e_im, v_re32, precision=HIGH) - jnp.einsum(
            "xtc,lt->lxc", e_re, v_im32, precision=HIGH
        )
        kgrad = jnp.stack([kg_re, kg_im]).reshape(2, kg_re.shape[0], readout, depth, ky_rows)
        zgrad = jnp.einsum("plxkr,pqzk->qlzxr", kgrad, inv_z, precision=HIGH).astype(jnp.bfloat16)
        back = lax.all_to_all(zgrad, "cuts", split_axis=2, concat_axis=4, tiled=True)
        return ((finish(back, maps, grad_acc), factor_acc + jnp.stack([gv_re, gv_im])), None)

    start_state = (
        jnp.zeros(basis.shape, jnp.float32),
        jnp.zeros((2, basis.shape[1], frames), jnp.float32),
    )
    inputs = (coil_maps.transpose(1, 0, 2, 3, 4), kdata.transpose(3, 0, 1, 2, 4))
    (grad_acc, factor_acc), unused = lax.scan(coil_step, start_state, inputs)
    shared = lax.psum_scatter(factor_acc * scale, "frame", scatter_dimension=2, tiled=True)
    factor_grad = lax.psum(shared, "cuts")
    return (grad_acc, factor_grad)


def solution(mesh):
    placed = (
        P(None, None, "cuts", "frame", None),
        P(None, None, "cuts", "frame", None),
        P(None, None, "frame"),
        P(None, "cuts"),
        P(None, None, "cuts", None, "frame"),
    )
    return jax.shard_map(
        body,
        mesh=mesh,
        in_specs=placed,
        out_specs=(P(None, None, "cuts", "frame", None), P(None, None, "frame")),
        check_vma=False,
    )
```

profile of v0, /device:TPU:0, one launch (start us, length us, event | category | flops | bytes accessed | tf_op | source)
XLA Modules:
  0.0 969.2 jit_solution(9303458574597565671)
XLA Ops:
  23.5 538.5 %while.15 = (s32[]{:T(128)}, f32[2,32,2,1,256]{4,1,0,2,3:T(8,128)S(1)}, f32[2,32,64]{2,1,0:T(8,128)S(1)}, bf16[12,2,2,1,256]{4,2,3,1,0:T(2,128)(2,1)S(1)}, f32[3...) while((s32[]{:T(128)}, ...), condition=%wide.region_1.2_spmd.clone.clone.clone, body=%wide.region_0.1_spmd.clone.clone.clone.sunk | while | flops 338577408 | bytes 9754888 | solution.py:119
  24.8 10.3 %all-to-all-start = ((bf16[64,2,256]{2,1,0:T(2,128)(2,1)}), bf16[64,2,256]{2,1,0:T(2,128)(2,1)S(1)}, u32[]{:S(2)}, u32[]{:S(2)}) async-start(bf16[64,2,256]{2,1,0:T(2,128)(2,1)} %reshape.531), calls=%async_computation | async-start | bytes 131072 | tf_op jit(solution)/shard_map/while/body/eval_jaxpr/all_to_all | solution.py:80
  35.1 10.0 %all-to-all-done = bf16[64,2,256]{2,1,0:T(2,128)(2,1)S(1)} async-done(((bf16[64,2,256]{2,1,0:T(2,128)(2,1)}), bf16[64,2,256]{2,1,0:T(2,128)(2,1)S(1)}, u32[]{:S(2)}, u32[]{:S(2)}) %all-to-all-start) | async-done | bytes 65568 | tf_op jit(solution)/shard_map/while/body/eval_jaxpr/all_to_all | solution.py:80
  62.7 10.0 %all-to-all-done.1 = bf16[64,2,256]{2,1,0:T(2,128)(2,1)S(1)} async-done(((bf16[64,2,256]{2,1,0:T(2,128)(2,1)}), bf16[64,2,256]{2,1,0:T(2,128)(2,1)S(1)}, u32[]{:S(2)}, u32[]{:S(2)}) %all-to-all-start.1) | async-done | bytes 65568 | tf_op jit(solution)/shard_map/while/body/eval_jaxpr/all_to_all | solution.py:111
  79.5 10.0 %all-to-all-done = bf16[64,2,256]{2,1,0:T(2,128)(2,1)S(1)} async-done(((bf16[64,2,256]{2,1,0:T(2,128)(2,1)}), bf16[64,2,256]{2,1,0:T(2,128)(2,1)S(1)}, u32[]{:S(2)}, u32[]{:S(2)}) %all-to-all-start) | async-done | bytes 65568 | tf_op jit(solution)/shard_map/while/body/eval_jaxpr/all_to_all | solution.py:80
  107.0 10.0 %all-to-all-done.1 = bf16[64,2,256]{2,1,0:T(2,128)(2,1)S(1)} async-done(((bf16[64,2,256]{2,1,0:T(2,128)(2,1)}), bf16[64,2,256]{2,1,0:T(2,128)(2,1)S(1)}, u32[]{:S(2)}, u32[]{:S(2)}) %all-to-all-start.1) | async-done | bytes 65568 | tf_op jit(solution)/shard_map/while/body/eval_jaxpr/all_to_all | solution.py:111
  123.8 10.0 %all-to-all-done = bf16[64,2,256]{2,1,0:T(2,128)(2,1)S(1)} async-done(((bf16[64,2,256]{2,1,0:T(2,128)(2,1)}), bf16[64,2,256]{2,1,0:T(2,128)(2,1)S(1)}, u32[]{:S(2)}, u32[]{:S(2)}) %all-to-all-start) | async-done | bytes 65568 | tf_op jit(solution)/shard_map/while/body/eval_jaxpr/all_to_all | solution.py:80
  151.3 10.0 %all-to-all-done.1 = bf16[64,2,256]{2,1,0:T(2,128)(2,1)S(1)} async-done(((bf16[64,2,256]{2,1,0:T(2,128)(2,1)}), bf16[64,2,256]{2,1,0:T(2,128)(2,1)S(1)}, u32[]{:S(2)}, u32[]{:S(2)}) %all-to-all-start.1) | async-done | bytes 65568 | tf_op jit(solution)/shard_map/while/body/eval_jaxpr/all_to_all | solution.py:111
  168.2 10.0 %all-to-all-done = bf16[64,2,256]{2,1,0:T(2,128)(2,1)S(1)} async-done(((bf16[64,2,256]{2,1,0:T(2,128)(2,1)}), bf16[64,2,256]{2,1,0:T(2,128)(2,1)S(1)}, u32[]{:S(2)}, u32[]{:S(2)}) %all-to-all-start) | async-done | bytes 65568 | tf_op jit(solution)/shard_map/while/body/eval_jaxpr/all_to_all | solution.py:80
  195.7 10.0 %all-to-all-done.1 = bf16[64,2,256]{2,1,0:T(2,128)(2,1)S(1)} async-done(((bf16[64,2,256]{2,1,0:T(2,128)(2,1)}), bf16[64,2,256]{2,1,0:T(2,128)(2,1)S(1)}, u32[]{:S(2)}, u32[]{:S(2)}) %all-to-all-start.1) | async-done | bytes 65568 | tf_op jit(solution)/shard_map/while/body/eval_jaxpr/all_to_all | solution.py:111
  212.5 10.0 %all-to-all-done = bf16[64,2,256]{2,1,0:T(2,128)(2,1)S(1)} async-done(((bf16[64,2,256]{2,1,0:T(2,128)(2,1)}), bf16[64,2,256]{2,1,0:T(2,128)(2,1)S(1)}, u32[]{:S(2)}, u32[]{:S(2)}) %all-to-all-start) | async-done | bytes 65568 | tf_op jit(solution)/shard_map/while/body/eval_jaxpr/all_to_all | solution.py:80
  240.0 10.0 %all-to-all-done.1 = bf16[64,2,256]{2,1,0:T(2,128)(2,1)S(1)} async-done(((bf16[64,2,256]{2,1,0:T(2,128)(2,1)}), bf16[64,2,256]{2,1,0:T(2,128)(2,1)S(1)}, u32[]{:S(2)}, u32[]{:S(2)}) %all-to-all-start.1) | async-done | bytes 65568 | tf_op jit(solution)/shard_map/while/body/eval_jaxpr/all_to_all | solution.py:111
  256.8 10.0 %all-to-all-done = bf16[64,2,256]{2,1,0:T(2,128)(2,1)S(1)} async-done(((bf16[64,2,256]{2,1,0:T(2,128)(2,1)}), bf16[64,2,256]{2,1,0:T(2,128)(2,1)S(1)}, u32[]{:S(2)}, u32[]{:S(2)}) %all-to-all-start) | async-done | bytes 65568 | tf_op jit(solution)/shard_map/while/body/eval_jaxpr/all_to_all | solution.py:80
  284.4 10.0 %all-to-all-done.1 = bf16[64,2,256]{2,1,0:T(2,128)(2,1)S(1)} async-done(((bf16[64,2,256]{2,1,0:T(2,128)(2,1)}), bf16[64,2,256]{2,1,0:T(2,128)(2,1)S(1)}, u32[]{:S(2)}, u32[]{:S(2)}) %all-to-all-start.1) | async-done | bytes 65568 | tf_op jit(solution)/shard_map/while/body/eval_jaxpr/all_to_all | solution.py:111
  301.2 10.0 %all-to-all-done = bf16[64,2,256]{2,1,0:T(2,128)(2,1)S(1)} async-done(((bf16[64,2,256]{2,1,0:T(2,128)(2,1)}), bf16[64,2,256]{2,1,0:T(2,128)(2,1)S(1)}, u32[]{:S(2)}, u32[]{:S(2)}) %all-to-all-start) | async-done | bytes 65568 | tf_op jit(solution)/shard_map/while/body/eval_jaxpr/all_to_all | solution.py:80
  328.7 10.4 %all-to-all-done.1 = bf16[64,2,256]{2,1,0:T(2,128)(2,1)S(1)} async-done(((bf16[64,2,256]{2,1,0:T(2,128)(2,1)}), bf16[64,2,256]{2,1,0:T(2,128)(2,1)S(1)}, u32[]{:S(2)}, u32[]{:S(2)}) %all-to-all-start.1) | async-done | bytes 65568 | tf_op jit(solution)/shard_map/while/body/eval_jaxpr/all_to_all | solution.py:111
  346.0 10.0 %all-to-all-done = bf16[64,2,256]{2,1,0:T(2,128)(2,1)S(1)} async-done(((bf16[64,2,256]{2,1,0:T(2,128)(2,1)}), bf16[64,2,256]{2,1,0:T(2,128)(2,1)S(1)}, u32[]{:S(2)}, u32[]{:S(2)}) %all-to-all-start) | async-done | bytes 65568 | tf_op jit(solution)/shard_map/while/body/eval_jaxpr/all_to_all | solution.py:80
  373.5 10.0 %all-to-all-done.1 = bf16[64,2,256]{2,1,0:T(2,128)(2,1)S(1)} async-done(((bf16[64,2,256]{2,1,0:T(2,128)(2,1)}), bf16[64,2,256]{2,1,0:T(2,128)(2,1)S(1)}, u32[]{:S(2)}, u32[]{:S(2)}) %all-to-all-start.1) | async-done | bytes 65568 | tf_op jit(solution)/shard_map/while/body/eval_jaxpr/all_to_all | solution.py:111
  390.3 10.0 %all-to-all-done = bf16[64,2,256]{2,1,0:T(2,128)(2,1)S(1)} async-done(((bf16[64,2,256]{2,1,0:T(2,128)(2,1)}), bf16[64,2,256]{2,1,0:T(2,128)(2,1)S(1)}, u32[]{:S(2)}, u32[]{:S(2)}) %all-to-all-start) | async-done | bytes 65568 | tf_op jit(solution)/shard_map/while/body/eval_jaxpr/all_to_all | solution.py:80
  434.7 10.0 %all-to-all-done = bf16[64,2,256]{2,1,0:T(2,128)(2,1)S(1)} async-done(((bf16[64,2,256]{2,1,0:T(2,128)(2,1)}), bf16[64,2,256]{2,1,0:T(2,128)(2,1)S(1)}, u32[]{:S(2)}, u32[]{:S(2)}) %all-to-all-start) | async-done | bytes 65568 | tf_op jit(solution)/shard_map/while/body/eval_jaxpr/all_to_all | solution.py:80
  479.0 10.0 %all-to-all-done = bf16[64,2,256]{2,1,0:T(2,128)(2,1)S(1)} async-done(((bf16[64,2,256]{2,1,0:T(2,128)(2,1)}), bf16[64,2,256]{2,1,0:T(2,128)(2,1)S(1)}, u32[]{:S(2)}, u32[]{:S(2)}) %all-to-all-start) | async-done | bytes 65568 | tf_op jit(solution)/shard_map/while/body/eval_jaxpr/all_to_all | solution.py:80
  523.4 10.0 %all-to-all-done = bf16[64,2,256]{2,1,0:T(2,128)(2,1)S(1)} async-done(((bf16[64,2,256]{2,1,0:T(2,128)(2,1)}), bf16[64,2,256]{2,1,0:T(2,128)(2,1)S(1)}, u32[]{:S(2)}, u32[]{:S(2)}) %all-to-all-start) | async-done | bytes 65568 | tf_op jit(solution)/shard_map/while/body/eval_jaxpr/all_to_all | solution.py:80
  563.6 30.3 %reduce-scatter.4.cloned.1.call-done = f32[16,64]{1,0:T(8,128)} async-done(((f32[64,64]{1,0:T(8,128)}), f32[16,64]{1,0:T(8,128)}) %reduce-scatter.4.cloned.1.call-update) | async-done | bytes 4112
  594.8 366.9 %psum.7 = f32[2,32,16]{2,1,0:T(8,128)S(1)} all-reduce(f32[2,32,16]{2,1,0:T(8,128)S(1)} %copy.183), channel_id=1, replica_groups=mesh['cuts'=64,'frame'=4] {'cuts'}, use_global_device_ids=true, to_apply=%region_3.4 | all-reduce | flops 1024 | bytes 8192 | tf_op jit(solution)/shard_map/psum | solution.py:121
  (625 shorter events, 343.8 us)
Async XLA Ops:
  7.2 586.8 %reduce-scatter.4.cloned.1.call-start = ((), (), s32[]{:S(2)}) async-start(), calls=%async_computation.3 | async-start | bytes 40960
  24.8 20.3 %all-to-all-start = ((bf16[64,2,256]{2,1,0:T(2,128)(2,1)}), bf16[64,2,256]{2,1,0:T(2,128)(2,1)S(1)}, u32[]{:S(2)}, u32[]{:S(2)}) async-start(bf16[64,2,256]{2,1,0:T(2,128)(2,1)} %reshape.531), calls=%async_computation | async-start | bytes 131072 | tf_op jit(solution)/shard_map/while/body/eval_jaxpr/all_to_all | solution.py:80
  58.0 14.6 %all-to-all-start.1 = ((bf16[64,2,256]{2,1,0:T(2,128)(2,1)}), bf16[64,2,256]{2,1,0:T(2,128)(2,1)S(1)}, u32[]{:S(2)}, u32[]{:S(2)}) async-start(bf16[64,2,256]{2,1,0:T(2,128)(2,1)} %reshape.533), calls=%async_computation.1 | async-start | bytes 131072 | tf_op jit(solution)/shard_map/while/body/eval_jaxpr/all_to_all | solution.py:111
  74.8 14.6 %all-to-all-start = ((bf16[64,2,256]{2,1,0:T(2,128)(2,1)}), bf16[64,2,256]{2,1,0:T(2,128)(2,1)S(1)}, u32[]{:S(2)}, u32[]{:S(2)}) async-start(bf16[64,2,256]{2,1,0:T(2,128)(2,1)} %reshape.531), calls=%async_computation | async-start | bytes 131072 | tf_op jit(solution)/shard_map/while/body/eval_jaxpr/all_to_all | solution.py:80
  102.4 14.6 %all-to-all-start.1 = ((bf16[64,2,256]{2,1,0:T(2,128)(2,1)}), bf16[64,2,256]{2,1,0:T(2,128)(2,1)S(1)}, u32[]{:S(2)}, u32[]{:S(2)}) async-start(bf16[64,2,256]{2,1,0:T(2,128)(2,1)} %reshape.533), calls=%async_computation.1 | async-start | bytes 131072 | tf_op jit(solution)/shard_map/while/body/eval_jaxpr/all_to_all | solution.py:111
  119.2 14.6 %all-to-all-start = ((bf16[64,2,256]{2,1,0:T(2,128)(2,1)}), bf16[64,2,256]{2,1,0:T(2,128)(2,1)S(1)}, u32[]{:S(2)}, u32[]{:S(2)}) async-start(bf16[64,2,256]{2,1,0:T(2,128)(2,1)} %reshape.531), calls=%async_computation | async-start | bytes 131072 | tf_op jit(solution)/shard_map/while/body/eval_jaxpr/all_to_all | solution.py:80
  146.7 14.6 %all-to-all-start.1 = ((bf16[64,2,256]{2,1,0:T(2,128)(2,1)}), bf16[64,2,256]{2,1,0:T(2,128)(2,1)S(1)}, u32[]{:S(2)}, u32[]{:S(2)}) async-start(bf16[64,2,256]{2,1,0:T(2,128)(2,1)} %reshape.533), calls=%async_computation.1 | async-start | bytes 131072 | tf_op jit(solution)/shard_map/while/body/eval_jaxpr/all_to_all | solution.py:111
  163.5 14.6 %all-to-all-start = ((bf16[64,2,256]{2,1,0:T(2,128)(2,1)}), bf16[64,2,256]{2,1,0:T(2,128)(2,1)S(1)}, u32[]{:S(2)}, u32[]{:S(2)}) async-start(bf16[64,2,256]{2,1,0:T(2,128)(2,1)} %reshape.531), calls=%async_computation | async-start | bytes 131072 | tf_op jit(solution)/shard_map/while/body/eval_jaxpr/all_to_all | solution.py:80
  191.0 14.6 %all-to-all-start.1 = ((bf16[64,2,256]{2,1,0:T(2,128)(2,1)}), bf16[64,2,256]{2,1,0:T(2,128)(2,1)S(1)}, u32[]{:S(2)}, u32[]{:S(2)}) async-start(bf16[64,2,256]{2,1,0:T(2,128)(2,1)} %reshape.533), calls=%async_computation.1 | async-start | bytes 131072 | tf_op jit(solution)/shard_map/while/body/eval_jaxpr/all_to_all | solution.py:111
  207.9 14.6 %all-to-all-start = ((bf16[64,2,256]{2,1,0:T(2,128)(2,1)}), bf16[64,2,256]{2,1,0:T(2,128)(2,1)S(1)}, u32[]{:S(2)}, u32[]{:S(2)}) async-start(bf16[64,2,256]{2,1,0:T(2,128)(2,1)} %reshape.531), calls=%async_computation | async-start | bytes 131072 | tf_op jit(solution)/shard_map/while/body/eval_jaxpr/all_to_all | solution.py:80
  235.4 14.6 %all-to-all-start.1 = ((bf16[64,2,256]{2,1,0:T(2,128)(2,1)}), bf16[64,2,256]{2,1,0:T(2,128)(2,1)S(1)}, u32[]{:S(2)}, u32[]{:S(2)}) async-start(bf16[64,2,256]{2,1,0:T(2,128)(2,1)} %reshape.533), calls=%async_computation.1 | async-start | bytes 131072 | tf_op jit(solution)/shard_map/while/body/eval_jaxpr/all_to_all | solution.py:111
  252.2 14.6 %all-to-all-start = ((bf16[64,2,256]{2,1,0:T(2,128)(2,1)}), bf16[64,2,256]{2,1,0:T(2,128)(2,1)S(1)}, u32[]{:S(2)}, u32[]{:S(2)}) async-start(bf16[64,2,256]{2,1,0:T(2,128)(2,1)} %reshape.531), calls=%async_computation | async-start | bytes 131072 | tf_op jit(solution)/shard_map/while/body/eval_jaxpr/all_to_all | solution.py:80
  279.7 14.6 %all-to-all-start.1 = ((bf16[64,2,256]{2,1,0:T(2,128)(2,1)}), bf16[64,2,256]{2,1,0:T(2,128)(2,1)S(1)}, u32[]{:S(2)}, u32[]{:S(2)}) async-start(bf16[64,2,256]{2,1,0:T(2,128)(2,1)} %reshape.533), calls=%async_computation.1 | async-start | bytes 131072 | tf_op jit(solution)/shard_map/while/body/eval_jaxpr/all_to_all | solution.py:111
  296.6 14.6 %all-to-all-start = ((bf16[64,2,256]{2,1,0:T(2,128)(2,1)}), bf16[64,2,256]{2,1,0:T(2,128)(2,1)S(1)}, u32[]{:S(2)}, u32[]{:S(2)}) async-start(bf16[64,2,256]{2,1,0:T(2,128)(2,1)} %reshape.531), calls=%async_computation | async-start | bytes 131072 | tf_op jit(solution)/shard_map/while/body/eval_jaxpr/all_to_all | solution.py:80
  324.1 15.1 %all-to-all-start.1 = ((bf16[64,2,256]{2,1,0:T(2,128)(2,1)}), bf16[64,2,256]{2,1,0:T(2,128)(2,1)S(1)}, u32[]{:S(2)}, u32[]{:S(2)}) async-start(bf16[64,2,256]{2,1,0:T(2,128)(2,1)} %reshape.533), calls=%async_computation.1 | async-start | bytes 131072 | tf_op jit(solution)/shard_map/while/body/eval_jaxpr/all_to_all | solution.py:111
  341.4 14.6 %all-to-all-start = ((bf16[64,2,256]{2,1,0:T(2,128)(2,1)}), bf16[64,2,256]{2,1,0:T(2,128)(2,1)S(1)}, u32[]{:S(2)}, u32[]{:S(2)}) async-start(bf16[64,2,256]{2,1,0:T(2,128)(2,1)} %reshape.531), calls=%async_computation | async-start | bytes 131072 | tf_op jit(solution)/shard_map/while/body/eval_jaxpr/all_to_all | solution.py:80
  368.9 14.6 %all-to-all-start.1 = ((bf16[64,2,256]{2,1,0:T(2,128)(2,1)}), bf16[64,2,256]{2,1,0:T(2,128)(2,1)S(1)}, u32[]{:S(2)}, u32[]{:S(2)}) async-start(bf16[64,2,256]{2,1,0:T(2,128)(2,1)} %reshape.533), calls=%async_computation.1 | async-start | bytes 131072 | tf_op jit(solution)/shard_map/while/body/eval_jaxpr/all_to_all | solution.py:111
  385.7 14.6 %all-to-all-start = ((bf16[64,2,256]{2,1,0:T(2,128)(2,1)}), bf16[64,2,256]{2,1,0:T(2,128)(2,1)S(1)}, u32[]{:S(2)}, u32[]{:S(2)}) async-start(bf16[64,2,256]{2,1,0:T(2,128)(2,1)} %reshape.531), calls=%async_computation | async-start | bytes 131072 | tf_op jit(solution)/shard_map/while/body/eval_jaxpr/all_to_all | solution.py:80
  413.2 14.6 %all-to-all-start.1 = ((bf16[64,2,256]{2,1,0:T(2,128)(2,1)}), bf16[64,2,256]{2,1,0:T(2,128)(2,1)S(1)}, u32[]{:S(2)}, u32[]{:S(2)}) async-start(bf16[64,2,256]{2,1,0:T(2,128)(2,1)} %reshape.533), calls=%async_computation.1 | async-start | bytes 131072 | tf_op jit(solution)/shard_map/while/body/eval_jaxpr/all_to_all | solution.py:111
  430.1 14.6 %all-to-all-start = ((bf16[64,2,256]{2,1,0:T(2,128)(2,1)}), bf16[64,2,256]{2,1,0:T(2,128)(2,1)S(1)}, u32[]{:S(2)}, u32[]{:S(2)}) async-start(bf16[64,2,256]{2,1,0:T(2,128)(2,1)} %reshape.531), calls=%async_computation | async-start | bytes 131072 | tf_op jit(solution)/shard_map/while/body/eval_jaxpr/all_to_all | solution.py:80
  457.6 14.6 %all-to-all-start.1 = ((bf16[64,2,256]{2,1,0:T(2,128)(2,1)}), bf16[64,2,256]{2,1,0:T(2,128)(2,1)S(1)}, u32[]{:S(2)}, u32[]{:S(2)}) async-start(bf16[64,2,256]{2,1,0:T(2,128)(2,1)} %reshape.533), calls=%async_computation.1 | async-start | bytes 131072 | tf_op jit(solution)/shard_map/while/body/eval_jaxpr/all_to_all | solution.py:111
  474.4 14.6 %all-to-all-start = ((bf16[64,2,256]{2,1,0:T(2,128)(2,1)}), bf16[64,2,256]{2,1,0:T(2,128)(2,1)S(1)}, u32[]{:S(2)}, u32[]{:S(2)}) async-start(bf16[64,2,256]{2,1,0:T(2,128)(2,1)} %reshape.531), calls=%async_computation | async-start | bytes 131072 | tf_op jit(solution)/shard_map/while/body/eval_jaxpr/all_to_all | solution.py:80
  501.9 14.6 %all-to-all-start.1 = ((bf16[64,2,256]{2,1,0:T(2,128)(2,1)}), bf16[64,2,256]{2,1,0:T(2,128)(2,1)S(1)}, u32[]{:S(2)}, u32[]{:S(2)}) async-start(bf16[64,2,256]{2,1,0:T(2,128)(2,1)} %reshape.533), calls=%async_computation.1 | async-start | bytes 131072 | tf_op jit(solution)/shard_map/while/body/eval_jaxpr/all_to_all | solution.py:111
  546.3 14.9 %all-to-all-start.1 = ((bf16[64,2,256]{2,1,0:T(2,128)(2,1)}), bf16[64,2,256]{2,1,0:T(2,128)(2,1)S(1)}, u32[]{:S(2)}, u32[]{:S(2)}) async-start(bf16[64,2,256]{2,1,0:T(2,128)(2,1)} %reshape.533), calls=%async_computation.1 | async-start | bytes 131072 | tf_op jit(solution)/shard_map/while/body/eval_jaxpr/all_to_all | solution.py:111
  (6 other events, 18.3 us)
Sparse Core Ops, SparseCore 0:
  562.9 30.9 reduce-scatter.3
where the time goes:
time: 971 us; the launch traced here: 969 us
  blocking collectives  376 us (39%)
  waiting for transfers between devices  271 us (28%)
  matrix products  127 us (13%)
  starting transfers between devices  117 us (12%)
  local copies, waits for them, and re-layouts  56.9 us (6%)
  between operations  14.2 us (1%)
    psum x1, blocking collectives, body(): factor_grad = lax.psum(shared, 'cuts')  367 us
    all_to_all x12, waiting for transfers between devices, coil_step(): lax.all_to_all(zgrad, 'cuts', split_axis=2, concat_axis=4, tiled=True)  120 us
    all_to_all x12, waiting for transfers between devices, coil_step(): lax.all_to_all(hybrid, 'cuts', split_axis=4, concat_axis=2, tiled=True)  120 us
    all_to_all x12, starting transfers between devices, coil_step(): lax.all_to_all(hybrid, 'cuts', split_axis=4, concat_axis=2, tiled=True)  61.1 us
    all_to_all x12, starting transfers between devices, coil_step(): lax.all_to_all(zgrad, 'cuts', split_axis=2, concat_axis=4, tiled=True)  55.6 us
    unnamed x2, waiting for transfers between devices  30.4 us
    dot_general x12, matrix products, coil_step(): pred_re = jnp.einsum('tsc,xtc->tsx', onehot32, mixed_re, precision=HIGH)  25 us
    dot_general x12, matrix products, coil_step(): pred_im = jnp.einsum('tsc,xtc->tsx', onehot32, mixed_im, precision=HIGH)  25 us
  transfers between devices with their start and end apart: 25, of which 25 were waited for; matrix products, arithmetic and copies ran while one was open for 0% of the time, Pallas kernels for 0%

commit v1 on v0

--- a/solution.py
+++ b/solution.py
@@ -118,7 +118,7 @@
     inputs = (coil_maps.transpose(1, 0, 2, 3, 4), kdata.transpose(3, 0, 1, 2, 4))
     (grad_acc, factor_acc), unused = lax.scan(coil_step, start_state, inputs)
     shared = lax.psum_scatter(factor_acc * scale, "frame", scatter_dimension=2, tiled=True)
-    factor_grad = lax.psum(shared, "cuts")
+    factor_grad = jnp.sum(lax.all_gather(shared, "cuts"), axis=0)
     return (grad_acc, factor_grad)
 
 

time: 971 us -> 769 us (0.79)
  blocking collectives: 376 us -> 218 us
  waiting for transfers between devices: 271 us -> 241 us
  between operations: 14.2 us -> 1.48 us
    psum x1 -> x0, blocking collectives: 367 us -> none  [body(): factor_grad = lax.psum(shared, 'cuts')]
    all_gather x0 -> x1, blocking collectives: none -> 190 us  [body(): factor_grad = jnp.sum(lax.all_gather(shared, 'cuts'), axis=0)]
    unnamed x2 -> x0, waiting for transfers between devices: 30.4 us -> none
    unnamed x0 -> x1, blocking collectives: none -> 18.5 us
  transfers between devices with their start and end apart: 25 -> 24, of which waited for: 25 -> 24; matrix products, arithmetic and copies ran while one was open for 0% -> 0% of each run, Pallas kernels for 0% -> 0%
where the time goes in v1:
time: 769 us; the launch traced here: 768 us
  waiting for transfers between devices  241 us (31%)
  blocking collectives  218 us (28%)
  matrix products  127 us (17%)
  starting transfers between devices  116 us (15%)
  local copies, waits for them, and re-layouts  56 us (7%)
    all_gather x1, blocking collectives, body(): factor_grad = jnp.sum(lax.all_gather(shared, 'cuts'), axis=0)  190 us
    all_to_all x12, waiting for transfers between devices, coil_step(): lax.all_to_all(hybrid, 'cuts', split_axis=4, concat_axis=2, tiled=True)  120 us
    all_to_all x12, waiting for transfers between devices, coil_step(): lax.all_to_all(zgrad, 'cuts', split_axis=2, concat_axis=4, tiled=True)  120 us
    all_to_all x12, starting transfers between devices, coil_step(): lax.all_to_all(hybrid, 'cuts', split_axis=4, concat_axis=2, tiled=True)  61.1 us
    all_to_all x12, starting transfers between devices, coil_step(): lax.all_to_all(zgrad, 'cuts', split_axis=2, concat_axis=4, tiled=True)  55.4 us
    dot_general x12, matrix products, coil_step(): pred_im = jnp.einsum('tsc,xtc->tsx', onehot32, mixed_im, precision=HIGH)  25 us
    dot_general x12, matrix products, coil_step(): pred_re = jnp.einsum('tsc,xtc->tsx', onehot32, mixed_re, precision=HIGH)  25 us
    while x48, local copies, waits for them, and re-layouts  24.2 us
  transfers between devices with their start and end apart: 24, of which 24 were waited for; matrix products, arithmetic and copies ran while one was open for 0% of the time, Pallas kernels for 0%

profile of v1, /device:TPU:0, one launch (start us, length us, event | category | flops | bytes accessed | tf_op | source)
XLA Modules:
  0.0 767.7 jit_solution(14587164778347933835)
XLA Ops:
  17.0 538.5 %while.15 = (s32[]{:T(128)}, f32[2,32,2,1,256]{4,1,0,2,3:T(8,128)S(1)}, f32[2,32,64]{2,1,0:T(8,128)S(1)}, bf16[12,2,2,1,256]{4,2,3,1,0:T(2,128)(2,1)S(1)}, f32[3...) while((s32[]{:T(128)}, ...), condition=%wide.region_1.2_spmd.clone.clone.clone, body=%wide.region_0.1_spmd.clone.clone.clone.sunk | while | flops 338577408 | bytes 9754888 | solution.py:119
  18.4 10.3 %all-to-all-start = ((bf16[64,2,256]{2,1,0:T(2,128)(2,1)}), bf16[64,2,256]{2,1,0:T(2,128)(2,1)S(1)}, u32[]{:S(2)}, u32[]{:S(2)}) async-start(bf16[64,2,256]{2,1,0:T(2,128)(2,1)} %reshape.531), calls=%async_computation | async-start | bytes 131072 | tf_op jit(solution)/shard_map/while/body/eval_jaxpr/all_to_all | solution.py:80
  28.7 10.0 %all-to-all-done = bf16[64,2,256]{2,1,0:T(2,128)(2,1)S(1)} async-done(((bf16[64,2,256]{2,1,0:T(2,128)(2,1)}), bf16[64,2,256]{2,1,0:T(2,128)(2,1)S(1)}, u32[]{:S(2)}, u32[]{:S(2)}) %all-to-all-start) | async-done | bytes 65568 | tf_op jit(solution)/shard_map/while/body/eval_jaxpr/all_to_all | solution.py:80
  56.2 10.0 %all-to-all-done.1 = bf16[64,2,256]{2,1,0:T(2,128)(2,1)S(1)} async-done(((bf16[64,2,256]{2,1,0:T(2,128)(2,1)}), bf16[64,2,256]{2,1,0:T(2,128)(2,1)S(1)}, u32[]{:S(2)}, u32[]{:S(2)}) %all-to-all-start.1) | async-done | bytes 65568 | tf_op jit(solution)/shard_map/while/body/eval_jaxpr/all_to_all | solution.py:111
  73.0 10.0 %all-to-all-done = bf16[64,2,256]{2,1,0:T(2,128)(2,1)S(1)} async-done(((bf16[64,2,256]{2,1,0:T(2,128)(2,1)}), bf16[64,2,256]{2,1,0:T(2,128)(2,1)S(1)}, u32[]{:S(2)}, u32[]{:S(2)}) %all-to-all-start) | async-done | bytes 65568 | tf_op jit(solution)/shard_map/while/body/eval_jaxpr/all_to_all | solution.py:80
  100.6 10.0 %all-to-all-done.1 = bf16[64,2,256]{2,1,0:T(2,128)(2,1)S(1)} async-done(((bf16[64,2,256]{2,1,0:T(2,128)(2,1)}), bf16[64,2,256]{2,1,0:T(2,128)(2,1)S(1)}, u32[]{:S(2)}, u32[]{:S(2)}) %all-to-all-start.1) | async-done | bytes 65568 | tf_op jit(solution)/shard_map/while/body/eval_jaxpr/all_to_all | solution.py:111
  117.4 10.0 %all-to-all-done = bf16[64,2,256]{2,1,0:T(2,128)(2,1)S(1)} async-done(((bf16[64,2,256]{2,1,0:T(2,128)(2,1)}), bf16[64,2,256]{2,1,0:T(2,128)(2,1)S(1)}, u32[]{:S(2)}, u32[]{:S(2)}) %all-to-all-start) | async-done | bytes 65568 | tf_op jit(solution)/shard_map/while/body/eval_jaxpr/all_to_all | solution.py:80
  144.9 10.0 %all-to-all-done.1 = bf16[64,2,256]{2,1,0:T(2,128)(2,1)S(1)} async-done(((bf16[64,2,256]{2,1,0:T(2,128)(2,1)}), bf16[64,2,256]{2,1,0:T(2,128)(2,1)S(1)}, u32[]{:S(2)}, u32[]{:S(2)}) %all-to-all-start.1) | async-done | bytes 65568 | tf_op jit(solution)/shard_map/while/body/eval_jaxpr/all_to_all | solution.py:111
  161.7 10.0 %all-to-all-done = bf16[64,2,256]{2,1,0:T(2,128)(2,1)S(1)} async-done(((bf16[64,2,256]{2,1,0:T(2,128)(2,1)}), bf16[64,2,256]{2,1,0:T(2,128)(2,1)S(1)}, u32[]{:S(2)}, u32[]{:S(2)}) %all-to-all-start) | async-done | bytes 65568 | tf_op jit(solution)/shard_map/while/body/eval_jaxpr/all_to_all | solution.py:80
  189.2 10.0 %all-to-all-done.1 = bf16[64,2,256]{2,1,0:T(2,128)(2,1)S(1)} async-done(((bf16[64,2,256]{2,1,0:T(2,128)(2,1)}), bf16[64,2,256]{2,1,0:T(2,128)(2,1)S(1)}, u32[]{:S(2)}, u32[]{:S(2)}) %all-to-all-start.1) | async-done | bytes 65568 | tf_op jit(solution)/shard_map/while/body/eval_jaxpr/all_to_all | solution.py:111
  206.0 10.0 %all-to-all-done = bf16[64,2,256]{2,1,0:T(2,128)(2,1)S(1)} async-done(((bf16[64,2,256]{2,1,0:T(2,128)(2,1)}), bf16[64,2,256]{2,1,0:T(2,128)(2,1)S(1)}, u32[]{:S(2)}, u32[]{:S(2)}) %all-to-all-start) | async-done | bytes 65568 | tf_op jit(solution)/shard_map/while/body/eval_jaxpr/all_to_all | solution.py:80
  233.6 10.0 %all-to-all-done.1 = bf16[64,2,256]{2,1,0:T(2,128)(2,1)S(1)} async-done(((bf16[64,2,256]{2,1,0:T(2,128)(2,1)}), bf16[64,2,256]{2,1,0:T(2,128)(2,1)S(1)}, u32[]{:S(2)}, u32[]{:S(2)}) %all-to-all-start.1) | async-done | bytes 65568 | tf_op jit(solution)/shard_map/while/body/eval_jaxpr/all_to_all | solution.py:111
  250.4 10.0 %all-to-all-done = bf16[64,2,256]{2,1,0:T(2,128)(2,1)S(1)} async-done(((bf16[64,2,256]{2,1,0:T(2,128)(2,1)}), bf16[64,2,256]{2,1,0:T(2,128)(2,1)S(1)}, u32[]{:S(2)}, u32[]{:S(2)}) %all-to-all-start) | async-done | bytes 65568 | tf_op jit(solution)/shard_map/while/body/eval_jaxpr/all_to_all | solution.py:80
  277.9 10.0 %all-to-all-done.1 = bf16[64,2,256]{2,1,0:T(2,128)(2,1)S(1)} async-done(((bf16[64,2,256]{2,1,0:T(2,128)(2,1)}), bf16[64,2,256]{2,1,0:T(2,128)(2,1)S(1)}, u32[]{:S(2)}, u32[]{:S(2)}) %all-to-all-start.1) | async-done | bytes 65568 | tf_op jit(solution)/shard_map/while/body/eval_jaxpr/all_to_all | solution.py:111
  294.7 10.0 %all-to-all-done = bf16[64,2,256]{2,1,0:T(2,128)(2,1)S(1)} async-done(((bf16[64,2,256]{2,1,0:T(2,128)(2,1)}), bf16[64,2,256]{2,1,0:T(2,128)(2,1)S(1)}, u32[]{:S(2)}, u32[]{:S(2)}) %all-to-all-start) | async-done | bytes 65568 | tf_op jit(solution)/shard_map/while/body/eval_jaxpr/all_to_all | solution.py:80
  322.3 10.4 %all-to-all-done.1 = bf16[64,2,256]{2,1,0:T(2,128)(2,1)S(1)} async-done(((bf16[64,2,256]{2,1,0:T(2,128)(2,1)}), bf16[64,2,256]{2,1,0:T(2,128)(2,1)S(1)}, u32[]{:S(2)}, u32[]{:S(2)}) %all-to-all-start.1) | async-done | bytes 65568 | tf_op jit(solution)/shard_map/while/body/eval_jaxpr/all_to_all | solution.py:111
  339.5 10.0 %all-to-all-done = bf16[64,2,256]{2,1,0:T(2,128)(2,1)S(1)} async-done(((bf16[64,2,256]{2,1,0:T(2,128)(2,1)}), bf16[64,2,256]{2,1,0:T(2,128)(2,1)S(1)}, u32[]{:S(2)}, u32[]{:S(2)}) %all-to-all-start) | async-done | bytes 65568 | tf_op jit(solution)/shard_map/while/body/eval_jaxpr/all_to_all | solution.py:80
  367.0 10.0 %all-to-all-done.1 = bf16[64,2,256]{2,1,0:T(2,128)(2,1)S(1)} async-done(((bf16[64,2,256]{2,1,0:T(2,128)(2,1)}), bf16[64,2,256]{2,1,0:T(2,128)(2,1)S(1)}, u32[]{:S(2)}, u32[]{:S(2)}) %all-to-all-start.1) | async-done | bytes 65568 | tf_op jit(solution)/shard_map/while/body/eval_jaxpr/all_to_all | solution.py:111
  383.8 10.0 %all-to-all-done = bf16[64,2,256]{2,1,0:T(2,128)(2,1)S(1)} async-done(((bf16[64,2,256]{2,1,0:T(2,128)(2,1)}), bf16[64,2,256]{2,1,0:T(2,128)(2,1)S(1)}, u32[]{:S(2)}, u32[]{:S(2)}) %all-to-all-start) | async-done | bytes 65568 | tf_op jit(solution)/shard_map/while/body/eval_jaxpr/all_to_all | solution.py:80
  428.1 10.0 %all-to-all-done = bf16[64,2,256]{2,1,0:T(2,128)(2,1)S(1)} async-done(((bf16[64,2,256]{2,1,0:T(2,128)(2,1)}), bf16[64,2,256]{2,1,0:T(2,128)(2,1)S(1)}, u32[]{:S(2)}, u32[]{:S(2)}) %all-to-all-start) | async-done | bytes 65568 | tf_op jit(solution)/shard_map/while/body/eval_jaxpr/all_to_all | solution.py:80
  472.5 10.0 %all-to-all-done = bf16[64,2,256]{2,1,0:T(2,128)(2,1)S(1)} async-done(((bf16[64,2,256]{2,1,0:T(2,128)(2,1)}), bf16[64,2,256]{2,1,0:T(2,128)(2,1)S(1)}, u32[]{:S(2)}, u32[]{:S(2)}) %all-to-all-start) | async-done | bytes 65568 | tf_op jit(solution)/shard_map/while/body/eval_jaxpr/all_to_all | solution.py:80
  516.8 10.3 %all-to-all-done = bf16[64,2,256]{2,1,0:T(2,128)(2,1)S(1)} async-done(((bf16[64,2,256]{2,1,0:T(2,128)(2,1)}), bf16[64,2,256]{2,1,0:T(2,128)(2,1)S(1)}, u32[]{:S(2)}, u32[]{:S(2)}) %all-to-all-start) | async-done | bytes 65568 | tf_op jit(solution)/shard_map/while/body/eval_jaxpr/all_to_all | solution.py:80
  555.6 18.5 %all-reduce = f32[2,32,64]{1,0,2:T(2,128)S(1)} all-reduce(f32[2,32,64]{1,0,2:T(2,128)S(1)} %copy.131), channel_id=3, replica_groups=mesh['cuts'=64,'frame'=4] {'frame'}, use_global_device_ids=true, to_apply=%region_2.3.clone | all-reduce | flops 4096 | bytes 32768
  576.1 190.1 %all-gather = f32[128,32,16]{1,2,0:T(8,128)S(1)} all-gather(f32[2,32,16]{1,2,0:T(8,128)S(1)} %copy.132), channel_id=2, replica_groups=mesh['cuts'=64,'frame'=4] {'cuts'}, dimensions={0}, use_global_device_ids=true | all-gather | bytes 266240 | tf_op jit(solution)/shard_map/all_gather | solution.py:121
  (625 shorter events, 343.3 us)
Async XLA Ops:
  18.4 20.3 %all-to-all-start = ((bf16[64,2,256]{2,1,0:T(2,128)(2,1)}), bf16[64,2,256]{2,1,0:T(2,128)(2,1)S(1)}, u32[]{:S(2)}, u32[]{:S(2)}) async-start(bf16[64,2,256]{2,1,0:T(2,128)(2,1)} %reshape.531), calls=%async_computation | async-start | bytes 131072 | tf_op jit(solution)/shard_map/while/body/eval_jaxpr/all_to_all | solution.py:80
  51.6 14.6 %all-to-all-start.1 = ((bf16[64,2,256]{2,1,0:T(2,128)(2,1)}), bf16[64,2,256]{2,1,0:T(2,128)(2,1)S(1)}, u32[]{:S(2)}, u32[]{:S(2)}) async-start(bf16[64,2,256]{2,1,0:T(2,128)(2,1)} %reshape.533), calls=%async_computation.1 | async-start | bytes 131072 | tf_op jit(solution)/shard_map/while/body/eval_jaxpr/all_to_all | solution.py:111
  68.4 14.6 %all-to-all-start = ((bf16[64,2,256]{2,1,0:T(2,128)(2,1)}), bf16[64,2,256]{2,1,0:T(2,128)(2,1)S(1)}, u32[]{:S(2)}, u32[]{:S(2)}) async-start(bf16[64,2,256]{2,1,0:T(2,128)(2,1)} %reshape.531), calls=%async_computation | async-start | bytes 131072 | tf_op jit(solution)/shard_map/while/body/eval_jaxpr/all_to_all | solution.py:80
  95.9 14.6 %all-to-all-start.1 = ((bf16[64,2,256]{2,1,0:T(2,128)(2,1)}), bf16[64,2,256]{2,1,0:T(2,128)(2,1)S(1)}, u32[]{:S(2)}, u32[]{:S(2)}) async-start(bf16[64,2,256]{2,1,0:T(2,128)(2,1)} %reshape.533), calls=%async_computation.1 | async-start | bytes 131072 | tf_op jit(solution)/shard_map/while/body/eval_jaxpr/all_to_all | solution.py:111
  112.7 14.6 %all-to-all-start = ((bf16[64,2,256]{2,1,0:T(2,128)(2,1)}), bf16[64,2,256]{2,1,0:T(2,128)(2,1)S(1)}, u32[]{:S(2)}, u32[]{:S(2)}) async-start(bf16[64,2,256]{2,1,0:T(2,128)(2,1)} %reshape.531), calls=%async_computation | async-start | bytes 131072 | tf_op jit(solution)/shard_map/while/body/eval_jaxpr/all_to_all | solution.py:80
  140.2 14.6 %all-to-all-start.1 = ((bf16[64,2,256]{2,1,0:T(2,128)(2,1)}), bf16[64,2,256]{2,1,0:T(2,128)(2,1)S(1)}, u32[]{:S(2)}, u32[]{:S(2)}) async-start(bf16[64,2,256]{2,1,0:T(2,128)(2,1)} %reshape.533), calls=%async_computation.1 | async-start | bytes 131072 | tf_op jit(solution)/shard_map/while/body/eval_jaxpr/all_to_all | solution.py:111
  157.1 14.6 %all-to-all-start = ((bf16[64,2,256]{2,1,0:T(2,128)(2,1)}), bf16[64,2,256]{2,1,0:T(2,128)(2,1)S(1)}, u32[]{:S(2)}, u32[]{:S(2)}) async-start(bf16[64,2,256]{2,1,0:T(2,128)(2,1)} %reshape.531), calls=%async_computation | async-start | bytes 131072 | tf_op jit(solution)/shard_map/while/body/eval_jaxpr/all_to_all | solution.py:80
  184.6 14.6 %all-to-all-start.1 = ((bf16[64,2,256]{2,1,0:T(2,128)(2,1)}), bf16[64,2,256]{2,1,0:T(2,128)(2,1)S(1)}, u32[]{:S(2)}, u32[]{:S(2)}) async-start(bf16[64,2,256]{2,1,0:T(2,128)(2,1)} %reshape.533), calls=%async_computation.1 | async-start | bytes 131072 | tf_op jit(solution)/shard_map/while/body/eval_jaxpr/all_to_all | solution.py:111
  201.4 14.6 %all-to-all-start = ((bf16[64,2,256]{2,1,0:T(2,128)(2,1)}), bf16[64,2,256]{2,1,0:T(2,128)(2,1)S(1)}, u32[]{:S(2)}, u32[]{:S(2)}) async-start(bf16[64,2,256]{2,1,0:T(2,128)(2,1)} %reshape.531), calls=%async_computation | async-start | bytes 131072 | tf_op jit(solution)/shard_map/while/body/eval_jaxpr/all_to_all | solution.py:80
  228.9 14.6 %all-to-all-start.1 = ((bf16[64,2,256]{2,1,0:T(2,128)(2,1)}), bf16[64,2,256]{2,1,0:T(2,128)(2,1)S(1)}, u32[]{:S(2)}, u32[]{:S(2)}) async-start(bf16[64,2,256]{2,1,0:T(2,128)(2,1)} %reshape.533), calls=%async_computation.1 | async-start | bytes 131072 | tf_op jit(solution)/shard_map/while/body/eval_jaxpr/all_to_all | solution.py:111
  245.7 14.6 %all-to-all-start = ((bf16[64,2,256]{2,1,0:T(2,128)(2,1)}), bf16[64,2,256]{2,1,0:T(2,128)(2,1)S(1)}, u32[]{:S(2)}, u32[]{:S(2)}) async-start(bf16[64,2,256]{2,1,0:T(2,128)(2,1)} %reshape.531), calls=%async_computation | async-start | bytes 131072 | tf_op jit(solution)/shard_map/while/body/eval_jaxpr/all_to_all | solution.py:80
  273.3 14.7 %all-to-all-start.1 = ((bf16[64,2,256]{2,1,0:T(2,128)(2,1)}), bf16[64,2,256]{2,1,0:T(2,128)(2,1)S(1)}, u32[]{:S(2)}, u32[]{:S(2)}) async-start(bf16[64,2,256]{2,1,0:T(2,128)(2,1)} %reshape.533), calls=%async_computation.1 | async-start | bytes 131072 | tf_op jit(solution)/shard_map/while/body/eval_jaxpr/all_to_all | solution.py:111
  290.1 14.6 %all-to-all-start = ((bf16[64,2,256]{2,1,0:T(2,128)(2,1)}), bf16[64,2,256]{2,1,0:T(2,128)(2,1)S(1)}, u32[]{:S(2)}, u32[]{:S(2)}) async-start(bf16[64,2,256]{2,1,0:T(2,128)(2,1)} %reshape.531), calls=%async_computation | async-start | bytes 131072 | tf_op jit(solution)/shard_map/while/body/eval_jaxpr/all_to_all | solution.py:80
  317.6 15.0 %all-to-all-start.1 = ((bf16[64,2,256]{2,1,0:T(2,128)(2,1)}), bf16[64,2,256]{2,1,0:T(2,128)(2,1)S(1)}, u32[]{:S(2)}, u32[]{:S(2)}) async-start(bf16[64,2,256]{2,1,0:T(2,128)(2,1)} %reshape.533), calls=%async_computation.1 | async-start | bytes 131072 | tf_op jit(solution)/shard_map/while/body/eval_jaxpr/all_to_all | solution.py:111
  334.8 14.6 %all-to-all-start = ((bf16[64,2,256]{2,1,0:T(2,128)(2,1)}), bf16[64,2,256]{2,1,0:T(2,128)(2,1)S(1)}, u32[]{:S(2)}, u32[]{:S(2)}) async-start(bf16[64,2,256]{2,1,0:T(2,128)(2,1)} %reshape.531), calls=%async_computation | async-start | bytes 131072 | tf_op jit(solution)/shard_map/while/body/eval_jaxpr/all_to_all | solution.py:80
  362.3 14.6 %all-to-all-start.1 = ((bf16[64,2,256]{2,1,0:T(2,128)(2,1)}), bf16[64,2,256]{2,1,0:T(2,128)(2,1)S(1)}, u32[]{:S(2)}, u32[]{:S(2)}) async-start(bf16[64,2,256]{2,1,0:T(2,128)(2,1)} %reshape.533), calls=%async_computation.1 | async-start | bytes 131072 | tf_op jit(solution)/shard_map/while/body/eval_jaxpr/all_to_all | solution.py:111
  379.2 14.6 %all-to-all-start = ((bf16[64,2,256]{2,1,0:T(2,128)(2,1)}), bf16[64,2,256]{2,1,0:T(2,128)(2,1)S(1)}, u32[]{:S(2)}, u32[]{:S(2)}) async-start(bf16[64,2,256]{2,1,0:T(2,128)(2,1)} %reshape.531), calls=%async_computation | async-start | bytes 131072 | tf_op jit(solution)/shard_map/while/body/eval_jaxpr/all_to_all | solution.py:80
  406.7 14.6 %all-to-all-start.1 = ((bf16[64,2,256]{2,1,0:T(2,128)(2,1)}), bf16[64,2,256]{2,1,0:T(2,128)(2,1)S(1)}, u32[]{:S(2)}, u32[]{:S(2)}) async-start(bf16[64,2,256]{2,1,0:T(2,128)(2,1)} %reshape.533), calls=%async_computation.1 | async-start | bytes 131072 | tf_op jit(solution)/shard_map/while/body/eval_jaxpr/all_to_all | solution.py:111
  423.5 14.6 %all-to-all-start = ((bf16[64,2,256]{2,1,0:T(2,128)(2,1)}), bf16[64,2,256]{2,1,0:T(2,128)(2,1)S(1)}, u32[]{:S(2)}, u32[]{:S(2)}) async-start(bf16[64,2,256]{2,1,0:T(2,128)(2,1)} %reshape.531), calls=%async_computation | async-start | bytes 131072 | tf_op jit(solution)/shard_map/while/body/eval_jaxpr/all_to_all | solution.py:80
  451.0 14.6 %all-to-all-start.1 = ((bf16[64,2,256]{2,1,0:T(2,128)(2,1)}), bf16[64,2,256]{2,1,0:T(2,128)(2,1)S(1)}, u32[]{:S(2)}, u32[]{:S(2)}) async-start(bf16[64,2,256]{2,1,0:T(2,128)(2,1)} %reshape.533), calls=%async_computation.1 | async-start | bytes 131072 | tf_op jit(solution)/shard_map/while/body/eval_jaxpr/all_to_all | solution.py:111
  467.8 14.6 %all-to-all-start = ((bf16[64,2,256]{2,1,0:T(2,128)(2,1)}), bf16[64,2,256]{2,1,0:T(2,128)(2,1)S(1)}, u32[]{:S(2)}, u32[]{:S(2)}) async-start(bf16[64,2,256]{2,1,0:T(2,128)(2,1)} %reshape.531), calls=%async_computation | async-start | bytes 131072 | tf_op jit(solution)/shard_map/while/body/eval_jaxpr/all_to_all | solution.py:80
  495.4 14.6 %all-to-all-start.1 = ((bf16[64,2,256]{2,1,0:T(2,128)(2,1)}), bf16[64,2,256]{2,1,0:T(2,128)(2,1)S(1)}, u32[]{:S(2)}, u32[]{:S(2)}) async-start(bf16[64,2,256]{2,1,0:T(2,128)(2,1)} %reshape.533), calls=%async_computation.1 | async-start | bytes 131072 | tf_op jit(solution)/shard_map/while/body/eval_jaxpr/all_to_all | solution.py:111
  512.2 15.0 %all-to-all-start = ((bf16[64,2,256]{2,1,0:T(2,128)(2,1)}), bf16[64,2,256]{2,1,0:T(2,128)(2,1)S(1)}, u32[]{:S(2)}, u32[]{:S(2)}) async-start(bf16[64,2,256]{2,1,0:T(2,128)(2,1)} %reshape.531), calls=%async_computation | async-start | bytes 131072 | tf_op jit(solution)/shard_map/while/body/eval_jaxpr/all_to_all | solution.py:80
  540.0 14.6 %all-to-all-start.1 = ((bf16[64,2,256]{2,1,0:T(2,128)(2,1)}), bf16[64,2,256]{2,1,0:T(2,128)(2,1)S(1)}, u32[]{:S(2)}, u32[]{:S(2)}) async-start(bf16[64,2,256]{2,1,0:T(2,128)(2,1)} %reshape.533), calls=%async_computation.1 | async-start | bytes 131072 | tf_op jit(solution)/shard_map/while/body/eval_jaxpr/all_to_all | solution.py:111
  (6 other events, 4.4 us)
